TPU v7x, 256 devices: a whole 4x4x8 slice. The times are simulated.
256 devices in a mesh: grp: 8 (over y, core), pan: 32 (over z, x).
Axes of the slice: x: 4, y: 4, z: 8, core: 2. Of those that a mesh axis runs over, the one named last changes fastest.
Arguments:
- anc_rows: bfloat16 [16384, 16384], P('grp', 'pan'), as said below
- row_home: int32 [128], replicated, may hold values from 0 to 127, as said below
- block_lists: int32 [8, 64], replicated, may hold values from 0 to 127, as said below
- front_blocks: int32 [8], replicated, may hold values from 32 to 64, as said below
- panel: bfloat16 [8, 8192, 768], P('grp', 'pan'), may hold values from -0.29882812 to 0.29882812
- pivot_inverse: bfloat16 [8, 768, 768], P('grp'), as said below
Outputs:
- cross_cov: bfloat16 [8, 8192, 768], P('grp', 'pan')
- pivot_cov: float32 [8, 768, 768], P('grp', 'pan')
Inputs may be any that keep to these rules, and one draw needn't show every extreme that they name: `row_home`: A permutation of 0 to 127; the 4 index blocks of each window [4 q, 4 q + 4) have their storage row blocks in one front group. `block_lists`: rising along each row; entries 2 * q to 2 * q + 1 lie in [4 * q, 4 * q + 4). `front_blocks`: some front has all 64 blocks. `anc_rows`: storage row block row_home[b] holds row block b of a symmetric matrix. `pivot_inverse`: lower triangular.
All inputs are finite; a program needn't handle non-finite values.
Results may differ from a plain program's by a relative error of at most 0.0095.
Values may be sent and summed in bfloat16 or wider, within the bound.
A program may use at most 128 MiB of HBM per device.

v0:
```python
import jax
import jax.numpy as jnp
from jax import lax
from jax.sharding import PartitionSpec as P

BLK = 128
P_SIZE = 768


def per_device(anc_rows, row_home, block_lists, front_blocks, panel, pivot_inverse):
    groups = lax.axis_size("grp")
    pan_count = lax.axis_size("pan")
    group_idx = lax.axis_index("grp")
    pan_idx = lax.axis_index("pan")
    block_count = row_home.shape[0]
    front_len = block_lists.shape[1]
    rb_local = front_len // pan_count
    cb_local = anc_rows.shape[1] // BLK
    stored_blocks = anc_rows.shape[0] // BLK
    windows = block_count // cb_local
    win_per_group = windows // groups
    per_src = win_per_group * rb_local
    contract = (((0,), (0,)), ((), ()))
    home_of_window = row_home[cb_local * jnp.arange(windows, dtype=jnp.int32)] // stored_blocks
    win = jnp.argsort(home_of_window * windows + jnp.arange(windows, dtype=jnp.int32))
    win = win.reshape(groups, win_per_group).astype(jnp.int32)
    pos = (rb_local * win[:, :, None] + jnp.arange(rb_local, dtype=jnp.int32)).reshape(
        groups, per_src
    )
    my_pos = lax.dynamic_index_in_dim(pos, group_idx, 0, keepdims=False)
    row_blocks = jnp.take(block_lists, my_pos, axis=1)
    slots = jnp.take(row_home, row_blocks) - stored_blocks * group_idx
    cols = (
        lax.dynamic_slice_in_dim(block_lists, rb_local * pan_idx, rb_local, axis=1)
        - cb_local * pan_idx
    )
    local = anc_rows.reshape(stored_blocks, BLK, cb_local, BLK)
    outgoing = local[slots[:, :, None], :, cols[:, None, :], :]
    received = lax.all_to_all(outgoing, "grp", split_axis=0, concat_axis=0, tiled=True)
    order = jnp.argsort(pos.reshape(groups * per_src)).astype(jnp.int32)
    sigma = jnp.take(received.reshape(groups * per_src, rb_local, BLK, BLK), order, axis=0)
    my_blocks = pan_idx * rb_local + jnp.arange(rb_local, dtype=jnp.int32)
    front_live = lax.dynamic_index_in_dim(front_blocks, group_idx, 0, keepdims=False)
    alive_rows = jnp.repeat(my_blocks < front_live, BLK)
    inverse_pivot = pivot_inverse[0]
    scaled = jnp.dot(panel[0], inverse_pivot, preferred_element_type=jnp.float32)
    scaled = jnp.where(alive_rows[:, None], scaled, jnp.zeros_like(scaled)).astype(jnp.bfloat16)
    full = lax.all_gather(scaled, "pan", axis=0, tiled=True)
    product = lax.dot_general(
        sigma,
        full.reshape(front_len, BLK, P_SIZE),
        (((0, 2), (0, 1)), ((), ())),
        preferred_element_type=jnp.float32,
    ).reshape(rb_local * BLK, P_SIZE)
    cross = jnp.where(alive_rows[:, None], -product, jnp.zeros_like(product)).astype(jnp.bfloat16)
    pivot_rows = P_SIZE // pan_count
    shared = lax.psum_scatter(
        (-lax.dot_general(scaled, cross, contract, preferred_element_type=jnp.float32)).astype(
            jnp.bfloat16
        ),
        "pan",
        scatter_dimension=0,
        tiled=True,
    ).astype(jnp.float32)
    own_columns = lax.dynamic_slice_in_dim(inverse_pivot, pan_idx * pivot_rows, pivot_rows, 1)
    triangle = lax.dot_general(
        own_columns, inverse_pivot, contract, preferred_element_type=jnp.float32
    )
    pivot = triangle + shared
    return (cross[None], pivot[None])


def solution(mesh):
    placed = (P("grp", "pan"), P(), P(), P(), P("grp", "pan", None), P("grp", None, None))
    return jax.shard_map(
        per_device,
        mesh=mesh,
        in_specs=placed,
        out_specs=(P("grp", "pan", None), P("grp", "pan", None)),
        check_vma=False,
    )
```

profile of v0, /device:TPU:8, one launch (start us, length us, event | category | flops | bytes accessed | tf_op | source)
XLA Modules:
  0.0 352.9 jit_solution(3056510419691765363)
XLA Ops:
  7.2 0.0 copy-start
  7.2 0.0 copy-start.1
  7.2 0.0 copy-start.4
  7.2 0.0 all-gather.2.cloned.1.call-start
  7.3 1.4 dynamic_slice.16
  8.7 0.7 add_compare_fusion
  9.3 0.1 broadcast_bitcast_fusion
  9.4 0.0 copy-done
  9.4 2.2 fusion.3
  11.6 0.0 all-gather.2.cloned.1.call-update
  11.7 1.4 gather_fusion
  13.1 1.6 sort.34
  14.7 0.1 mul.53
  14.7 0.1 copy.20
  14.8 0.1 add.144
  14.9 0.1 broadcast_add_fusion
  15.0 0.2 dynamic-slice_reduce_fusion
  15.2 0.8 copy.23
  16.0 0.6 gather_fusion.1
  16.5 0.1 copy.24
  16.6 0.1 reshape.182
  16.7 0.8 gather_fusion.2
  17.5 0.1 reshape.181
  17.6 0.1 copy.25
  17.6 0.1 fusion.17
  17.7 0.1 copy.26
  17.8 0.1 fusion.19
  17.9 0.1 broadcast_or_fusion
  18.0 0.1 reshape.188
  18.1 2.1 reshape.205
  20.2 2.1 copy.27
  22.4 3.1 gather_fusion.3
  25.4 6.6 %all-to-all-start = ((bf16[8,8,2,128,128]{4,3,2,1,0:T(8,128)(2,1)}), bf16[8,8,2,128,128]{4,3,2,1,0:T(8,128)(2,1)}, u32[]{:S(2)}, u32[]{:S(2)}) async-start(bf16[8,8,2,128,128]{4,3,2,1,0:T(8,128)(2,1)} %bitcast.59), calls=%async_computation | async-start | bytes 8388608 | tf_op jit(solution)/shard_map/all_to_all | solution.py:39
  32.1 0.0 reduce-scatter.2.cloned.1.call-start
  32.1 0.1 copy.21
  32.2 0.1 add.139
  32.3 2.0 sort.35
  34.4 46.0 %all-to-all-done = bf16[8,8,2,128,128]{4,3,2,1,0:T(8,128)(2,1)} async-done(((bf16[8,8,2,128,128]{4,3,2,1,0:T(8,128)(2,1)}), bf16[8,8,2,128,128]{4,3,2,1,0:T(8,128)(2,1)}, u32[]{:S(2)}, u32[]{:S(2)}) %all-to-all-start) | async-done | bytes 4194336 | tf_op jit(solution)/shard_map/all_to_all | solution.py:39
  80.4 5.2 %gather_fusion.4 = bf16[64,2,128,128]{3,2,1,0:T(8,128)(2,1)} fusion(bf16[64,2,128,128]{3,2,1,0:T(8,128)(2,1)} %bitcast.8, s32[1024]{0:T(1024)S(1)} %pad_clamp_fusion), kind=kCustom, calls=%fused_computation.4 | custom fusion | bytes 8388864 | tf_op jit(solution)/shard_map/jit(_take)/gather | solution.py:41
  85.7 4.5 %select_bitcast_fusion = bf16[2,128,64,128]{1,3,0,2:T(8,128)(2,1)} fusion(bf16[64,2,128,128]{3,2,1,0:T(8,128)(2,1)} %gather_fusion.4, pred[64]{0:T(512)(128)(4,1)S(1)} %compare_and_fusion.1), kind=kLoop, calls=%fused_computation.5 | loop fusion | flops 2097152 | bytes 8388672 | tf_op jit(solution)/shard_map/jit(_take)/select_n | solution.py:41
  90.2 6.4 %copy.32 = bf16[2,128,64,128]{3,1,0,2:T(8,128)(2,1)} copy(bf16[2,128,64,128]{1,3,0,2:T(8,128)(2,1)} %select_bitcast_fusion) | data formatting | bytes 8388608 | tf_op jit(solution)/shard_map/dot_general | solution.py:49
  96.6 37.7 %all-gather.2.cloned.1.call-done = bf16[8192,768]{1,0:T(8,128)(2,1)} async-done(((bf16[256,768]{1,0:T(8,128)(2,1)}), bf16[8192,768]{1,0:T(8,128)(2,1)}) %all-gather.2.cloned.1.call-update) | async-done | bytes 12582928 | tf_op jit(solution)/shard_map/all_gather | solution.py:48
  134.3 8.8 %fusion.2 = bf16[256,768]{1,0:T(8,128)(2,1)S(1)} fusion(bf16[256,64,128]{2,0,1:T(8,128)(2,1)} %bitcast.60, bf16[64,128,768]{2,1,0:T(8,128)(2,1)} %bitcast.63, pred[256]{0:T(512)(128)(4,1)S(1)} %broadcast_bitcast_fusion), kind=kOutput, calls=%fused_computation.11 | convolution fusion | flops 3221815296 | bytes 17170688 | tf_op jit(solution)/shard_map/dot_general | solution.py:49
  143.1 0.0 copy-start.5
  143.1 1.5 negate_convert_fusion
  144.7 0.0 reduce-scatter.2.cloned.1.call-update
  144.7 199.6 %reduce-scatter.2.cloned.1.call-done = bf16[24,768]{1,0:T(8,128)(2,1)} async-done(((bf16[768,768]{1,0:T(8,128)(2,1)}), bf16[24,768]{1,0:T(8,128)(2,1)}) %reduce-scatter.2.cloned.1.call-update) | async-done | bytes 36880 | tf_op jit(solution)/shard_map/reduce_scatter | solution.py:57
  344.3 1.8 fusion.10
  (24 shorter events, 0.1 us)
Async XLA Ops:
  7.2 2.2 copy-start
  7.2 9.5 %copy-start.1 = (s32[128]{0:T(128)S(1)}, s32[128]{0:T(128)}, u32[]{:S(2)}) copy-start(s32[128]{0:T(128)} %param.7) | copy-start | bytes 1540
  7.2 10.6 %copy-start.4 = (s32[8,64]{1,0:T(8,128)S(1)}, s32[8,64]{1,0:T(8,128)}, u32[]{:S(2)}) copy-start(s32[8,64]{1,0:T(8,128)} %param.8) | copy-start | bytes 6148
  7.2 10.9 %copy-start.2 = (bf16[2048,512]{1,0:T(8,128)(2,1)S(1)}, bf16[2048,512]{1,0:T(8,128)(2,1)}, u32[]{:S(2)}) copy-start(bf16[2048,512]{1,0:T(8,128)(2,1)} %param.6) | copy-start | bytes 6291460
  7.2 127.1 %all-gather.2.cloned.1.call-start = ((), (), s32[]{:S(2)}) async-start(), calls=%async_computation.2 | async-start | bytes 12976128 | tf_op jit(solution)/shard_map/all_gather | solution.py:48
  25.4 55.0 %all-to-all-start = ((bf16[8,8,2,128,128]{4,3,2,1,0:T(8,128)(2,1)}), bf16[8,8,2,128,128]{4,3,2,1,0:T(8,128)(2,1)}, u32[]{:S(2)}, u32[]{:S(2)}) async-start(bf16[8,8,2,128,128]{4,3,2,1,0:T(8,128)(2,1)} %bitcast.59), calls=%async_computation | async-start | bytes 8388608 | tf_op jit(solution)/shard_map/all_to_all | solution.py:39
  32.1 312.2 %reduce-scatter.2.cloned.1.call-start = ((), (), s32[]{:S(2)}) async-start(), calls=%async_computation.3 | async-start | bytes 1216512 | tf_op jit(solution)/shard_map/reduce_scatter | solution.py:57
  134.3 8.8 %copy-start.3 = (bf16[256,768]{1,0:T(8,128)(2,1)S(1)}, bf16[256,768]{1,0:T(8,128)(2,1)}, u32[]{:S(2)}) copy-start(bf16[256,768]{1,0:T(8,128)(2,1)} %fusion.3) | copy-start | bytes 1179652
  143.1 203.0 %copy-start.5 = (bf16[256,768]{1,0:T(8,128)(2,1)}, bf16[256,768]{1,0:T(8,128)(2,1)S(1)}, u32[]{:S(2)}) copy-start(bf16[256,768]{1,0:T(8,128)(2,1)S(1)} %fusion.2) | copy-start | bytes 1179652
Sparse Core Ops, SparseCore 0:
  11.8 122.4 all-gather.1
  144.8 199.4 reduce-scatter.1
where the time goes:
time: 353 us
  waiting for transfers between devices  283 us (80%)
  local copies, waits for them, and re-layouts  25.1 us (7%)
  matrix products  14.3 us (4%)
  between operations  14.2 us (4%)
  other arithmetic  9.24 us (3%)
  starting transfers between devices  6.68 us (2%)
    reduce_scatter x1, waiting for transfers between devices, per_device(): lax.psum_scatter((-lax.dot_general(scaled, cross, contract, preferred_ele...  200 us
    all_to_all x1, waiting for transfers between devices, per_device(): lax.all_to_all(outgoing, 'grp', split_axis=0, concat_axis=0, tiled=True)  46 us
    all_gather x1, waiting for transfers between devices, per_device(): full = lax.all_gather(scaled, 'pan', axis=0, tiled=True)  37.7 us
    dot_general x1, matrix products, per_device(): lax.dot_general(sigma, full.reshape(front_len, BLK, P_SIZE), (((0, 2), (0...  8.79 us
  transfers between devices with their start and end apart: 3, of which 3 were waited for; matrix products, arithmetic and copies ran while one was open for 9% of the time, Pallas kernels for 0%

commit v1 on v0

--- a/solution.py
+++ b/solution.py
@@ -45,7 +45,9 @@
     inverse_pivot = pivot_inverse[0]
     scaled = jnp.dot(panel[0], inverse_pivot, preferred_element_type=jnp.float32)
     scaled = jnp.where(alive_rows[:, None], scaled, jnp.zeros_like(scaled)).astype(jnp.bfloat16)
-    full = lax.all_gather(scaled, "pan", axis=0, tiled=True)
+    full = jnp.concatenate(
+        lax.all_to_all(jnp.stack([scaled] * lax.axis_size("pan")), "pan", 0, 0), axis=0
+    )
     product = lax.dot_general(
         sigma,
         full.reshape(front_len, BLK, P_SIZE),

time: 353 us -> 616 us (1.75)
  waiting for transfers between devices: 283 us -> 532 us
  starting transfers between devices: 6.68 us -> 16.5 us
    all_to_all x0 -> x1, waiting for transfers between devices: none -> 265 us  [per_device(): lax.all_to_all(jnp.stack([scaled] * lax.axis_size('pan')), 'pan', 0, 0)]
    all_gather x1 -> x0, waiting for transfers between devices: 37.7 us -> none  [per_device(): full = lax.all_gather(scaled, 'pan', axis=0, tiled=True)]
    reduce_scatter x1, waiting for transfers between devices: 200 us -> 220 us  [per_device(): lax.psum_scatter((-lax.dot_general(scaled, cross, contract, preferred_ele...]
    all_to_all x0 -> x1, starting transfers between devices: none -> 9.69 us  [per_device(): lax.all_to_all(jnp.stack([scaled] * lax.axis_size('pan')), 'pan', 0, 0)]
  transfers between devices with their start and end apart: 3 -> 3, of which waited for: 3 -> 3; matrix products, arithmetic and copies ran while one was open for 9% -> 3% of each run, Pallas kernels for 0% -> 0%
where the time goes in v1:
time: 616 us; the launch traced here: 615 us
  waiting for transfers between devices  532 us (86%)
  local copies, waits for them, and re-layouts  30.9 us (5%)
  starting transfers between devices  16.5 us (3%)
  between operations  14.2 us (2%)
  matrix products  12.7 us (2%)
  other arithmetic  9.26 us (2%)
    all_to_all x1, waiting for transfers between devices, per_device(): lax.all_to_all(jnp.stack([scaled] * lax.axis_size('pan')), 'pan', 0, 0)  265 us
    reduce_scatter x1, waiting for transfers between devices, per_device(): lax.psum_scatter((-lax.dot_general(scaled, cross, contract, preferred_ele...  220 us
    all_to_all x1, waiting for transfers between devices, per_device(): lax.all_to_all(outgoing, 'grp', split_axis=0, concat_axis=0, tiled=True)  46.5 us
  transfers between devices with their start and end apart: 3, of which 3 were waited for; matrix products, arithmetic and copies ran while one was open for 3% of the time, Pallas kernels for 0%

profile of v1, /device:TPU:8, one launch (start us, length us, event | category | flops | bytes accessed | tf_op | source)
XLA Modules:
  0.0 615.4 jit_solution(1720224530766737796)
XLA Ops:
  7.2 0.0 copy-start
  7.2 0.0 copy-start.2
  7.2 0.1 add.144
  7.3 1.5 gather_fusion
  8.9 1.6 sort.34
  10.5 0.1 mul.53
  10.6 0.1 copy.20
  10.7 0.1 broadcast_add_fusion
  10.7 0.2 dynamic-slice_reduce_fusion
  11.0 0.8 copy.23
  11.7 0.6 gather_fusion.1
  12.3 0.1 copy.24
  12.4 0.1 reshape.180
  12.5 1.4 gather_fusion.2
  13.9 0.1 reshape.179
  14.0 0.1 copy.25
  14.0 0.1 fusion.17
  14.1 0.1 copy.26
  14.2 0.1 fusion.19
  14.3 0.1 broadcast_or_fusion
  14.4 0.1 reshape.186
  14.5 0.0 copy-done.1
  14.5 2.1 reshape.203
  16.6 2.1 copy.27
  18.8 3.1 gather_fusion.3
  21.8 6.8 %all-to-all-start = ((bf16[8,8,2,128,128]{4,3,2,1,0:T(8,128)(2,1)}), bf16[8,8,2,128,128]{4,3,2,1,0:T(8,128)(2,1)}, u32[]{:S(2)}, u32[]{:S(2)}) async-start(bf16[8,8,2,128,128]{4,3,2,1,0:T(8,128)(2,1)} %bitcast.59), calls=%async_computation | async-start | bytes 8388608 | tf_op jit(solution)/shard_map/all_to_all | solution.py:39
  28.6 0.6 dynamic_slice.16
  29.2 0.7 add_compare_fusion
  29.9 0.1 broadcast_bitcast_fusion
  29.9 0.0 copy-done
  29.9 0.5 fusion.3
  30.4 46.5 %all-to-all-done = bf16[8,8,2,128,128]{4,3,2,1,0:T(8,128)(2,1)} async-done(((bf16[8,8,2,128,128]{4,3,2,1,0:T(8,128)(2,1)}), bf16[8,8,2,128,128]{4,3,2,1,0:T(8,128)(2,1)}, u32[]{:S(2)}, u32[]{:S(2)}) %all-to-all-start) | async-done | bytes 4194336 | tf_op jit(solution)/shard_map/all_to_all | solution.py:39
  77.0 5.9 stack.2
  82.9 9.7 %all-to-all-start.1 = ((bf16[32,256,768]{2,1,0:T(8,128)(2,1)}), bf16[32,256,768]{2,1,0:T(8,128)(2,1)}, u32[]{:S(2)}, u32[]{:S(2)}) async-start(bf16[32,256,768]{2,1,0:T(8,128)(2,1)} %stack.2), calls=%async_computation.1 | async-start | bytes 25165824 | tf_op jit(solution)/shard_map/all_to_all | solution.py:49
  92.6 0.0 reduce-scatter.2.cloned.1.call-start
  92.6 0.1 copy.21
  92.7 0.1 add.139
  92.8 2.0 sort.35
  94.9 5.2 gather_fusion.4
  100.1 4.6 select_bitcast_fusion
  104.7 6.3 %copy.32 = bf16[2,128,64,128]{3,1,0,2:T(8,128)(2,1)} copy(bf16[2,128,64,128]{1,3,0,2:T(8,128)(2,1)} %select_bitcast_fusion) | data formatting | bytes 8388608 | tf_op jit(solution)/shard_map/dot_general | solution.py:51
  111.1 264.8 %all-to-all-done.1 = bf16[32,256,768]{2,1,0:T(8,128)(2,1)} async-done(((bf16[32,256,768]{2,1,0:T(8,128)(2,1)}), bf16[32,256,768]{2,1,0:T(8,128)(2,1)}, u32[]{:S(2)}, u32[]{:S(2)}) %all-to-all-start.1) | async-done | bytes 12582944 | tf_op jit(solution)/shard_map/all_to_all | solution.py:49
  375.9 8.9 %fusion.2 = bf16[256,768]{1,0:T(8,128)(2,1)S(1)} fusion(bf16[256,64,128]{2,0,1:T(8,128)(2,1)} %bitcast.60, bf16[64,128,768]{2,1,0:T(8,128)(2,1)} %bitcast.14, pred[256]{0:T(512)(128)(4,1)S(1)} %broadcast_bitcast_fusion), kind=kOutput, calls=%fused_computation.11 | convolution fusion | flops 3221815296 | bytes 17170688 | tf_op jit(solution)/shard_map/dot_general | solution.py:51
  384.8 0.0 copy-start.5
  384.8 1.5 negate_convert_fusion
  386.3 0.0 reduce-scatter.2.cloned.1.call-update
  386.4 220.4 %reduce-scatter.2.cloned.1.call-done = bf16[24,768]{1,0:T(8,128)(2,1)} async-done(((bf16[768,768]{1,0:T(8,128)(2,1)}), bf16[24,768]{1,0:T(8,128)(2,1)}) %reduce-scatter.2.cloned.1.call-update) | async-done | bytes 36880 | tf_op jit(solution)/shard_map/reduce_scatter | solution.py:59
  606.8 1.8 fusion.10
  (24 shorter events, 0.1 us)
Async XLA Ops:
  7.2 22.8 %copy-start = (bf16[1,768,768]{2,1,0:T(8,128)(2,1)S(1)}, bf16[1,768,768]{2,1,0:T(8,128)(2,1)}, u32[]{:S(2)}) copy-start(bf16[1,768,768]{2,1,0:T(8,128)(2,1)} %param.11) | copy-start | bytes 3538948
  7.2 7.0 %copy-start.2 = (s32[8,64]{1,0:T(8,128)S(1)}, s32[8,64]{1,0:T(8,128)}, u32[]{:S(2)}) copy-start(s32[8,64]{1,0:T(8,128)} %param.8) | copy-start | bytes 6148
  7.2 7.3 %copy-start.1 = (bf16[2048,512]{1,0:T(8,128)(2,1)S(1)}, bf16[2048,512]{1,0:T(8,128)(2,1)}, u32[]{:S(2)}) copy-start(bf16[2048,512]{1,0:T(8,128)(2,1)} %param.6) | copy-start | bytes 6291460
  21.8 6.8 %copy-start.4 = (s32[8]{0:T(128)S(1)}, s32[8]{0:T(128)}, u32[]{:S(2)}) copy-start(s32[8]{0:T(128)} %param.9) | copy-start | bytes 100
  21.8 8.1 %copy-start.3 = (bf16[1,256,768]{2,1,0:T(8,128)(2,1)S(1)}, bf16[1,256,768]{2,1,0:T(8,128)(2,1)}, u32[]{:S(2)}) copy-start(bf16[1,256,768]{2,1,0:T(8,128)(2,1)} %param.10) | copy-start | bytes 1179652
  21.8 55.1 %all-to-all-start = ((bf16[8,8,2,128,128]{4,3,2,1,0:T(8,128)(2,1)}), bf16[8,8,2,128,128]{4,3,2,1,0:T(8,128)(2,1)}, u32[]{:S(2)}, u32[]{:S(2)}) async-start(bf16[8,8,2,128,128]{4,3,2,1,0:T(8,128)(2,1)} %bitcast.59), calls=%async_computation | async-start | bytes 8388608 | tf_op jit(solution)/shard_map/all_to_all | solution.py:39
  82.9 293.0 %all-to-all-start.1 = ((bf16[32,256,768]{2,1,0:T(8,128)(2,1)}), bf16[32,256,768]{2,1,0:T(8,128)(2,1)}, u32[]{:S(2)}, u32[]{:S(2)}) async-start(bf16[32,256,768]{2,1,0:T(8,128)(2,1)} %stack.2), calls=%async_computation.1 | async-start | bytes 25165824 | tf_op jit(solution)/shard_map/all_to_all | solution.py:49
  92.6 514.2 %reduce-scatter.2.cloned.1.call-start = ((), (), s32[]{:S(2)}) async-start(), calls=%async_computation.3 | async-start | bytes 1216512 | tf_op jit(solution)/shard_map/reduce_scatter | solution.py:59
  384.8 223.8 %copy-start.5 = (bf16[256,768]{1,0:T(8,128)(2,1)}, bf16[256,768]{1,0:T(8,128)(2,1)S(1)}, u32[]{:S(2)}) copy-start(bf16[256,768]{1,0:T(8,128)(2,1)S(1)} %fusion.2) | copy-start | bytes 1179652
Sparse Core Ops, SparseCore 0:
  386.5 220.2 reduce-scatter.1
